TPU v7x, 32 devices: a whole 2x2x4 slice. The times are simulated.
32 devices in a mesh: tm: 4 (over y, x), space: 8 (over z, core).
Axes of the slice: x: 2, y: 2, z: 4, core: 2. Of those that a mesh axis runs over, the one named last changes fastest.
Arguments:
- queries: bfloat16 [4, 768, 3072], P('tm', 'space'), may hold values from -8 to 8
- key_rows: bfloat16 [4, 768, 3072], P('tm', 'space'), may hold values from -8 to 8
- value_rows: bfloat16 [4, 768, 3072], P('tm', 'space'), may hold values from -6 to 6
- noise_level: int32 [4], P('tm'), may hold values from 0 to 999
- decay_power: int32 [24], replicated, may hold values from 0 to 7
- head_gain: float32 [24, 128], replicated, may hold values from 0.1 to 1.9
Outputs:
- attended: bfloat16 [4, 768, 3072], P('tm', 'space')
All inputs are finite; a program needn't handle non-finite values.
Results may differ from a plain program's by a relative error of at most 0.0049.
Values may be sent and summed in bfloat16 or wider, within the bound.
A program may use at most 64 MiB of HBM per device.

v0:
```python
import jax
import jax.numpy as jnp
from jax import lax
from jax.sharding import PartitionSpec as P

LEVELS = 1000
HGROUPS = 8
epsilon = 1e-06


def carried_in(value, axis, join, neutral):
    count, mine = (lax.axis_size(axis), lax.axis_index(axis))
    pieces = jax.tree.map(lambda part: lax.all_gather(part, axis), value)
    so_far = jax.tree.map(
        lambda part, zero: jnp.full_like(part, 0) + jnp.asarray(zero, part.dtype), value, neutral
    )

    def lap(position, so_far):
        longer = join(so_far, jax.tree.map(lambda part: part[position], pieces))
        return jax.tree.map(lambda new, old: jnp.where(position < mine, new, old), longer, so_far)

    return lax.fori_loop(0, count - 1, lap, so_far)


def spread_items(block, quarters, heads_total, depth):
    part_rows = block.shape[0] // quarters
    shaped = block.reshape(quarters, part_rows, heads_total, depth).transpose(0, 2, 1, 3)
    return shaped.reshape(quarters * heads_total, part_rows, depth)


def copied_items(block, quarters, heads_total, depth):
    every = block.reshape(block.shape[0], heads_total, depth).transpose(1, 0, 2)
    copied = jnp.broadcast_to(every[None], (quarters,) + every.shape)
    return copied.reshape(quarters * heads_total, block.shape[0], depth)


def attend_head(bundle):
    query, key_item, value_item, state, gain_row = bundle
    factor = query.shape[1] ** (-0.5)
    scores = jnp.dot(query, key_item.T, preferred_element_type=jnp.float32) * factor
    row_top = jnp.max(scores, axis=1, keepdims=True)
    weights = jnp.exp(scores - row_top)
    row_total = jnp.sum(weights, axis=1, keepdims=True)
    numerator = jnp.dot(
        weights.astype(jnp.bfloat16), value_item, preferred_element_type=jnp.float32
    )
    carried = jnp.dot(query, state, preferred_element_type=jnp.float32) * factor
    mixed = numerator / row_total + carried
    normed = mixed * lax.rsqrt(jnp.mean(mixed * mixed, axis=1, keepdims=True) + epsilon) * gain_row
    return normed.astype(jnp.bfloat16)


def compose(earlier, later):
    return (earlier[0] * later[0], later[0][:, None, None] * earlier[1] + later[1])


def body(queries, key_rows, value_rows, noise_level, decay_power, head_gain):
    heads_total = decay_power.shape[0]
    depth = head_gain.shape[1]
    local_rows = queries.shape[1]
    quarters = lax.axis_size("space") // HGROUPS
    grouped = heads_total // HGROUPS
    query_items = spread_items(queries[0], quarters, heads_total, depth)
    keys_sent = copied_items(key_rows[0], quarters, heads_total, depth)
    values_sent = copied_items(value_rows[0], quarters, heads_total, depth)
    query_got, keys_got, values_got = (
        lax.all_to_all(query_items, "space", split_axis=0, concat_axis=1, tiled=True),
        lax.all_to_all(keys_sent, "space", split_axis=0, concat_axis=1, tiled=True),
        lax.all_to_all(values_sent, "space", split_axis=0, concat_axis=1, tiled=True),
    )
    key_count = keys_got.shape[1]
    fresh = (
        jnp.einsum("inh,ine->ihe", keys_got, values_got, preferred_element_type=jnp.float32)
        / key_count
    )
    group_index = lax.axis_index("space") % HGROUPS
    powers = lax.dynamic_slice_in_dim(decay_power, group_index * grouped, grouped).astype(
        jnp.float32
    )
    level_now = noise_level[0].astype(jnp.float32)
    block_count = lax.axis_size("tm")
    rate = jnp.exp2(-(powers * (0.25 + 1.75 * level_now / LEVELS)) / block_count)
    zeros_state = jnp.zeros_like(fresh)
    unused_rate, before = carried_in(
        (rate, fresh), "tm", compose, (jnp.ones_like(rate), zeros_state)
    )
    state = (rate[:, None, None] * before).astype(jnp.bfloat16)
    gain_rows = lax.dynamic_slice_in_dim(head_gain, group_index * grouped, grouped)
    outcome = lax.map(attend_head, (query_got, keys_got, values_got, state, gain_rows))
    returned = lax.all_to_all(outcome, "space", split_axis=1, concat_axis=0, tiled=True)
    part_rows = local_rows // quarters
    restored = returned.reshape(quarters, heads_total, part_rows, depth).transpose(0, 2, 1, 3)
    return restored.reshape(1, local_rows, heads_total * depth)


def solution(mesh):
    in_specs = (
        P("tm", "space", None),
        P("tm", "space", None),
        P("tm", "space", None),
        P("tm"),
        P(),
        P(),
    )
    out_specs = P("tm", "space", None)
    return jax.shard_map(body, mesh=mesh, in_specs=in_specs, out_specs=out_specs, check_vma=False)
```

profile of v0, /device:TPU:0, one launch (start us, length us, event | category | flops | bytes accessed | tf_op | source)
XLA Modules:
  0.0 99.5 jit_solution(8693053812802755996)
XLA Ops:
  0.0 1.2 %copy.38 = bf16[12,8,24,128]{3,2,1,0:T(8,128)(2,1)S(1)} copy(bf16[12,8,24,128]{3,1,2,0:T(8,128)(2,1)} %bitcast.111) | data formatting | bytes 1179648
  1.2 0.9 copy.26
  2.2 6.5 %all-to-all-start.1 = ((bf16[24,96,128]{2,1,0:T(8,128)(2,1)}), bf16[24,96,128]{2,1,0:T(8,128)(2,1)S(1)}, u32[]{:S(2)}, u32[]{:S(2)}) async-start(bf16[24,96,128]{2,1,0:T(8,128)(2,1)} %copy.26), calls=%async_computation.1 | async-start | bytes 1179648 | tf_op jit(solution)/shard_map/all_to_all | solution.py:68
  8.8 0.9 copy.28
  9.7 15.7 %all-to-all-done.1 = bf16[24,96,128]{2,1,0:T(8,128)(2,1)S(1)} async-done(((bf16[24,96,128]{2,1,0:T(8,128)(2,1)}), bf16[24,96,128]{2,1,0:T(8,128)(2,1)S(1)}, u32[]{:S(2)}, u32[]{:S(2)}) %all-to-all-start.1) | async-done | bytes 589856 | tf_op jit(solution)/shard_map/all_to_all | solution.py:68
  25.4 3.5 %all-to-all-start.2 = ((bf16[24,96,128]{2,1,0:T(8,128)(2,1)}), bf16[24,96,128]{2,1,0:T(8,128)(2,1)S(1)}, u32[]{:S(2)}, u32[]{:S(2)}) async-start(bf16[24,96,128]{2,1,0:T(8,128)(2,1)} %copy.28), calls=%async_computation.2 | async-start | bytes 1179648 | tf_op jit(solution)/shard_map/all_to_all | solution.py:69
  29.6 0.6 dynamic-slice
  31.0 9.9 %all-reduce = f32[12]{0:T(128)S(1)} all-reduce(f32[12]{0:T(128)S(1)} %get-tuple-element.187), channel_id=2, replica_groups=mesh['tm'=4,'space'=8] {'tm'}, use_global_device_ids=true, to_apply=%add | all-reduce | flops 12 | bytes 96
  41.2 0.9 copy.24
  42.2 3.4 %all-to-all-done.2 = bf16[24,96,128]{2,1,0:T(8,128)(2,1)S(1)} async-done(((bf16[24,96,128]{2,1,0:T(8,128)(2,1)}), bf16[24,96,128]{2,1,0:T(8,128)(2,1)S(1)}, u32[]{:S(2)}, u32[]{:S(2)}) %all-to-all-start.2) | async-done | bytes 589856 | tf_op jit(solution)/shard_map/all_to_all | solution.py:69
  45.6 3.5 %all-to-all-start = ((bf16[24,96,128]{2,1,0:T(8,128)(2,1)}), bf16[24,96,128]{2,1,0:T(8,128)(2,1)S(1)}, u32[]{:S(2)}, u32[]{:S(2)}) async-start(bf16[24,96,128]{2,1,0:T(8,128)(2,1)} %copy.24), calls=%async_computation | async-start | bytes 1179648 | tf_op jit(solution)/shard_map/all_to_all | solution.py:67
  49.2 0.4 convolution_multiply_fusion.1
  49.5 12.5 %all-gather.1 = f32[12,128,128]{2,1,0:T(8,128)S(1)} all-gather(f32[3,128,128]{2,1,0:T(8,128)S(1)} %convolution_multiply_fusion.1), channel_id=3, replica_groups=mesh['tm'=4,'space'=8] {'tm'}, dimensions={0}, use_global_device_ids=true | all-gather | bytes 983040 | tf_op jit(solution)/shard_map/all_gather | solution.py:13
  62.1 0.4 while.25
  62.5 3.3 %all-to-all-done = bf16[24,96,128]{2,1,0:T(8,128)(2,1)S(1)} async-done(((bf16[24,96,128]{2,1,0:T(8,128)(2,1)}), bf16[24,96,128]{2,1,0:T(8,128)(2,1)S(1)}, u32[]{:S(2)}, u32[]{:S(2)}) %all-to-all-start) | async-done | bytes 589856 | tf_op jit(solution)/shard_map/all_to_all | solution.py:67
  65.9 7.7 %while.24 = (s32[]{:T(128)}, bf16[3,768,128]{1,2,0:T(8,128)(2,1)}, bf16[3,768,128]{2,1,0:T(8,128)(2,1)S(1)}, bf16[3,768,128]{2,1,0:T(8,128)(2,1)S(1)}, bf16[3,76...) while((s32[]{:T(128)}, bf16[3,768,128]{1,2,0:T(8,128)(2,1)}, ...), condition=%wide.region_6.7_spmd, body=%wide.region_2.6_spmd.sunk | while | flops 332659968 | bytes 9700445 | solution.py:89
  65.9 0.5 multiply_reduce_fusion.4
  66.4 0.4 fusion.36
  67.1 0.6 multiply_reduce_fusion.5
  67.7 0.8 fusion.38
  68.5 0.5 multiply_reduce_fusion.4
  69.0 0.4 fusion.36
  69.4 0.3 convolution_multiply_fusion.3
  69.7 0.6 multiply_reduce_fusion.5
  70.3 0.8 fusion.38
  71.0 0.5 multiply_reduce_fusion.4
  71.5 0.4 fusion.36
  72.2 0.6 multiply_reduce_fusion.5
  72.8 0.8 fusion.38
  73.6 1.5 %copy.31 = bf16[3,768,128]{2,0,1:T(4,128)(2,1)S(1)} copy(bf16[3,768,128]{1,2,0:T(8,128)(2,1)} %get-tuple-element.137) | data formatting | bytes 1179648 | tf_op jit(solution)/shard_map/while | solution.py:89
  75.1 23.4 %all_to_all.69 = bf16[3,768,128]{2,0,1:T(4,128)(2,1)S(1)} all-to-all(bf16[3,768,128]{2,0,1:T(4,128)(2,1)S(1)} %copy.31), channel_id=1, replica_groups=mesh['tm'=4,'space'=8] {'space'}, dimensions={1} | all-to-all | bytes 1179648 | tf_op jit(solution)/shard_map/all_to_all | solution.py:90
  98.6 1.0 copy.41
  (39 shorter events, 1.8 us)
Async XLA Ops:
  0.0 42.1 %copy-start = (f32[24,128]{1,0:T(8,128)S(1)}, f32[24,128]{1,0:T(8,128)}, u32[]{:S(2)}) copy-start(f32[24,128]{1,0:T(8,128)} %param.15) | copy-start | bytes 36868
  0.0 8.6 %copy-start.1 = (bf16[1,96,3072]{2,1,0:T(8,128)(2,1)S(1)}, bf16[1,96,3072]{2,1,0:T(8,128)(2,1)}, u32[]{:S(2)}) copy-start(bf16[1,96,3072]{2,1,0:T(8,128)(2,1)} %param.12) | copy-start | bytes 1769476
  2.1 27.4 %copy-start.4 = (u32[32]{0:T(128)S(1)}, u32[32]{0:T(128)}, u32[]{:S(2)}) copy-start(u32[32]{0:T(128)} %constant.102) | copy-start | bytes 388
  2.1 28.7 %copy-start.3 = (s32[24]{0:T(128)S(1)}, s32[24]{0:T(128)}, u32[]{:S(2)}) copy-start(s32[24]{0:T(128)} %param.14) | copy-start | bytes 292
  2.2 38.9 %copy-start.2 = (bf16[1,96,3072]{2,1,0:T(8,128)(2,1)S(1)}, bf16[1,96,3072]{2,1,0:T(8,128)(2,1)}, u32[]{:S(2)}) copy-start(bf16[1,96,3072]{2,1,0:T(8,128)(2,1)} %param.10) | copy-start | bytes 1769476
  2.2 23.2 %all-to-all-start.1 = ((bf16[24,96,128]{2,1,0:T(8,128)(2,1)}), bf16[24,96,128]{2,1,0:T(8,128)(2,1)S(1)}, u32[]{:S(2)}, u32[]{:S(2)}) async-start(bf16[24,96,128]{2,1,0:T(8,128)(2,1)} %copy.26), calls=%async_computation.1 | async-start | bytes 1179648 | tf_op jit(solution)/shard_map/all_to_all | solution.py:68
  25.4 20.2 %all-to-all-start.2 = ((bf16[24,96,128]{2,1,0:T(8,128)(2,1)}), bf16[24,96,128]{2,1,0:T(8,128)(2,1)S(1)}, u32[]{:S(2)}, u32[]{:S(2)}) async-start(bf16[24,96,128]{2,1,0:T(8,128)(2,1)} %copy.28), calls=%async_computation.2 | async-start | bytes 1179648 | tf_op jit(solution)/shard_map/all_to_all | solution.py:69
  45.6 20.2 %all-to-all-start = ((bf16[24,96,128]{2,1,0:T(8,128)(2,1)}), bf16[24,96,128]{2,1,0:T(8,128)(2,1)S(1)}, u32[]{:S(2)}, u32[]{:S(2)}) async-start(bf16[24,96,128]{2,1,0:T(8,128)(2,1)} %copy.24), calls=%async_computation | async-start | bytes 1179648 | tf_op jit(solution)/shard_map/all_to_all | solution.py:67
where the time goes:
time: 100 us; the launch traced here: 99.5 us
  blocking collectives  45.8 us (46%)
  waiting for transfers between devices  22.4 us (22%)
  starting transfers between devices  13.6 us (14%)
  local copies, waits for them, and re-layouts  7.68 us (8%)
  matrix products  4.3 us (4%)
  other arithmetic  4.18 us (4%)
  between operations  1.48 us (1%)
    all_to_all x1, blocking collectives, body(): lax.all_to_all(outcome, 'space', split_axis=1, concat_axis=0, tiled=True)  23.4 us
    all_to_all x1, waiting for transfers between devices, body(): lax.all_to_all(keys_sent, 'space', split_axis=0, concat_axis=1, tiled=True)  15.7 us
    all_gather x1, blocking collectives, carried_in(): pieces = jax.tree.map(lambda part: lax.all_gather(part, axis), value)  12.5 us
    unnamed x1, blocking collectives  9.88 us
    all_to_all x1, starting transfers between devices, body(): lax.all_to_all(keys_sent, 'space', split_axis=0, concat_axis=1, tiled=True)  6.49 us
    all_to_all x1, starting transfers between devices, body(): lax.all_to_all(values_sent, 'space', split_axis=0, concat_axis=1, tiled=T...  3.54 us
    all_to_all x1, starting transfers between devices, body(): lax.all_to_all(query_items, 'space', split_axis=0, concat_axis=1, tiled=T...  3.54 us
    all_to_all x1, waiting for transfers between devices, body(): lax.all_to_all(values_sent, 'space', split_axis=0, concat_axis=1, tiled=T...  3.4 us
  transfers between devices with their start and end apart: 3, of which 3 were waited for; matrix products, arithmetic and copies ran while one was open for 4% of the time, Pallas kernels for 0%

commit v1 on v0

--- a/solution.py
+++ b/solution.py
@@ -6,6 +6,18 @@
 LEVELS = 1000
 HGROUPS = 8
 epsilon = 1e-06
+
+
+def cut_along(shard, dim, size):
+    shape = shard.shape
+    blocks = shard.reshape(*shape[:dim], size, shape[dim] // size, *shape[dim + 1 :])
+    return jnp.moveaxis(blocks, dim, 0)
+
+
+def in_order(blocks, dim):
+    lengths = list(blocks.shape[1:])
+    lengths[dim] *= blocks.shape[0]
+    return jnp.moveaxis(blocks, 0, dim).reshape(lengths)
 
 
 def carried_in(value, axis, join, neutral):
@@ -87,7 +99,14 @@
     state = (rate[:, None, None] * before).astype(jnp.bfloat16)
     gain_rows = lax.dynamic_slice_in_dim(head_gain, group_index * grouped, grouped)
     outcome = lax.map(attend_head, (query_got, keys_got, values_got, state, gain_rows))
-    returned = lax.all_to_all(outcome, "space", split_axis=1, concat_axis=0, tiled=True)
+    size, index = (lax.axis_size("space"), lax.axis_index("space"))
+    blocks = cut_along(outcome, 1, size)
+    outs = [blocks[index]]
+    for step in range(1, size):
+        sent = blocks[index ^ step]
+        outs.append(lax.ppermute(sent, "space", [(i, i ^ step) for i in range(size)]))
+    blocks = jnp.stack(outs)[index ^ jnp.arange(size)]
+    returned = in_order(blocks, 0)
     part_rows = local_rows // quarters
     restored = returned.reshape(quarters, heads_total, part_rows, depth).transpose(0, 2, 1, 3)
     return restored.reshape(1, local_rows, heads_total * depth)

time: 100 us -> 93.3 us (0.933); the launches traced: 99.5 us -> 91.8 us
  blocking collectives: 45.8 us -> 22.4 us
  starting transfers between devices: 13.6 us -> 21.8 us
  waiting for transfers between devices: 22.4 us -> 28 us
  local copies, waits for them, and re-layouts: 7.68 us -> 11.4 us
  other arithmetic: 4.18 us -> 2.14 us
    all_to_all x1 -> x0, blocking collectives: 23.4 us -> none  [body(): lax.all_to_all(outcome, 'space', split_axis=1, concat_axis=0, tiled=True)]
    ppermute x0 -> x7, starting transfers between devices: none -> 8.23 us  [body(): lax.ppermute(sent, 'space', [(i, i ^ step) for i in range(size)])]
    ppermute x0 -> x7, waiting for transfers between devices: none -> 5.65 us  [body(): lax.ppermute(sent, 'space', [(i, i ^ step) for i in range(size)])]
    dynamic_update_slice x0 -> x6, local copies, waits for them, and re-layouts: none -> 2.57 us  [body(): lax.map(attend_head, (query_got, keys_got, values_got, state, gain_rows))]
    dynamic_update_slice x3 -> x0, other arithmetic: 2.32 us -> none  [body(): lax.map(attend_head, (query_got, keys_got, values_got, state, gain_rows))]
    while x1 -> x0, local copies, waits for them, and re-layouts: 1.47 us -> none  [body(): lax.map(attend_head, (query_got, keys_got, values_got, state, gain_rows))]
    squeeze x0 -> x1, local copies, waits for them, and re-layouts: none -> 1.14 us  [body(): sent = blocks[index ^ step]]
    unnamed x15 -> x22, local copies, waits for them, and re-layouts: 2.04 us -> 3.02 us
  transfers between devices with their start and end apart: 3 -> 10, of which waited for: 3 -> 5; matrix products, arithmetic and copies ran while one was open for 4% -> 5% of each run, Pallas kernels for 0% -> 0%
where the time goes in v1:
time: 93.3 us; the launch traced here: 91.8 us
  waiting for transfers between devices  28 us (30%)
  blocking collectives  22.4 us (24%)
  starting transfers between devices  21.8 us (23%)
  local copies, waits for them, and re-layouts  11.4 us (12%)
  matrix products  4.28 us (5%)
  other arithmetic  2.14 us (2%)
  between operations  1.57 us (2%)
    all_to_all x1, waiting for transfers between devices, body(): lax.all_to_all(keys_sent, 'space', split_axis=0, concat_axis=1, tiled=True)  15.7 us
    all_gather x1, blocking collectives, carried_in(): pieces = jax.tree.map(lambda part: lax.all_gather(part, axis), value)  12.5 us
    unnamed x1, blocking collectives  9.88 us
    ppermute x7, starting transfers between devices, body(): lax.ppermute(sent, 'space', [(i, i ^ step) for i in range(size)])  8.23 us
    all_to_all x1, starting transfers between devices, body(): lax.all_to_all(keys_sent, 'space', split_axis=0, concat_axis=1, tiled=True)  6.49 us
    ppermute x7, waiting for transfers between devices, body(): lax.ppermute(sent, 'space', [(i, i ^ step) for i in range(size)])  5.65 us
    all_to_all x1, starting transfers between devices, body(): lax.all_to_all(values_sent, 'space', split_axis=0, concat_axis=1, tiled=T...  3.54 us
    all_to_all x1, starting transfers between devices, body(): lax.all_to_all(query_items, 'space', split_axis=0, concat_axis=1, tiled=T...  3.54 us
  transfers between devices with their start and end apart: 10, of which 5 were waited for; matrix products, arithmetic and copies ran while one was open for 5% of the time, Pallas kernels for 0%

profile of v1, /device:TPU:0, one launch (start us, length us, event | category | flops | bytes accessed | tf_op | source)
XLA Modules:
  0.0 91.8 jit_solution(7260103150056672376)
XLA Ops:
  0.0 1.2 %copy.35 = bf16[12,8,24,128]{3,2,1,0:T(8,128)(2,1)S(1)} copy(bf16[12,8,24,128]{3,1,2,0:T(8,128)(2,1)} %bitcast.138) | data formatting | bytes 1179648
  1.2 0.9 copy.23
  2.2 6.5 %all-to-all-start.1 = ((bf16[24,96,128]{2,1,0:T(8,128)(2,1)}), bf16[24,96,128]{2,1,0:T(8,128)(2,1)S(1)}, u32[]{:S(2)}, u32[]{:S(2)}) async-start(bf16[24,96,128]{2,1,0:T(8,128)(2,1)} %copy.23), calls=%async_computation.1 | async-start | bytes 1179648 | tf_op jit(solution)/shard_map/all_to_all | solution.py:80
  8.8 0.9 copy.25
  9.7 15.7 %all-to-all-done.1 = bf16[24,96,128]{2,1,0:T(8,128)(2,1)S(1)} async-done(((bf16[24,96,128]{2,1,0:T(8,128)(2,1)}), bf16[24,96,128]{2,1,0:T(8,128)(2,1)S(1)}, u32[]{:S(2)}, u32[]{:S(2)}) %all-to-all-start.1) | async-done | bytes 589856 | tf_op jit(solution)/shard_map/all_to_all | solution.py:80
  25.4 3.5 %all-to-all-start.2 = ((bf16[24,96,128]{2,1,0:T(8,128)(2,1)}), bf16[24,96,128]{2,1,0:T(8,128)(2,1)S(1)}, u32[]{:S(2)}, u32[]{:S(2)}) async-start(bf16[24,96,128]{2,1,0:T(8,128)(2,1)} %copy.25), calls=%async_computation.2 | async-start | bytes 1179648 | tf_op jit(solution)/shard_map/all_to_all | solution.py:81
  29.6 0.6 dynamic-slice.32
  31.0 9.9 %all-reduce = f32[12]{0:T(128)S(1)} all-reduce(f32[12]{0:T(128)S(1)} %get-tuple-element.187), channel_id=2, replica_groups=mesh['tm'=4,'space'=8] {'tm'}, use_global_device_ids=true, to_apply=%add | all-reduce | flops 12 | bytes 96
  41.2 0.9 copy.21
  42.2 3.4 %all-to-all-done.2 = bf16[24,96,128]{2,1,0:T(8,128)(2,1)S(1)} async-done(((bf16[24,96,128]{2,1,0:T(8,128)(2,1)}), bf16[24,96,128]{2,1,0:T(8,128)(2,1)S(1)}, u32[]{:S(2)}, u32[]{:S(2)}) %all-to-all-start.2) | async-done | bytes 589856 | tf_op jit(solution)/shard_map/all_to_all | solution.py:81
  45.6 3.5 %all-to-all-start = ((bf16[24,96,128]{2,1,0:T(8,128)(2,1)}), bf16[24,96,128]{2,1,0:T(8,128)(2,1)S(1)}, u32[]{:S(2)}, u32[]{:S(2)}) async-start(bf16[24,96,128]{2,1,0:T(8,128)(2,1)} %copy.21), calls=%async_computation | async-start | bytes 1179648 | tf_op jit(solution)/shard_map/all_to_all | solution.py:79
  49.5 12.5 %all-gather.1 = f32[12,128,128]{2,1,0:T(8,128)S(1)} all-gather(f32[3,128,128]{2,1,0:T(8,128)S(1)} %convolution_multiply_fusion.1), channel_id=3, replica_groups=mesh['tm'=4,'space'=8] {'tm'}, dimensions={0}, use_global_device_ids=true | all-gather | bytes 983040 | tf_op jit(solution)/shard_map/all_gather | solution.py:25
  62.5 3.3 %all-to-all-done = bf16[24,96,128]{2,1,0:T(8,128)(2,1)S(1)} async-done(((bf16[24,96,128]{2,1,0:T(8,128)(2,1)}), bf16[24,96,128]{2,1,0:T(8,128)(2,1)S(1)}, u32[]{:S(2)}, u32[]{:S(2)}) %all-to-all-start) | async-done | bytes 589856 | tf_op jit(solution)/shard_map/all_to_all | solution.py:79
  65.9 8.2 %while.24 = (s32[]{:T(128)}, bf16[3,768,128]{2,1,0:T(8,128)(2,1)}, bf16[3,768,128]{2,1,0:T(8,128)(2,1)S(1)}, bf16[3,768,128]{2,1,0:T(8,128)(2,1)S(1)}, bf16[3,76...) while((s32[]{:T(128)}, bf16[3,768,128]{2,1,0:T(8,128)(2,1)}, ...), condition=%wide.region_6.7_spmd, body=%wide.region_2.6_spmd.sunk | while | flops 332659968 | bytes 10486877 | solution.py:101
  65.9 0.5 multiply_reduce_fusion.4
  67.1 0.6 multiply_reduce_fusion.5
  68.0 0.7 constant_dynamic-update-slice_fusion.2
  69.8 0.6 multiply_reduce_fusion.5
  70.7 0.7 constant_dynamic-update-slice_fusion.2
  71.4 0.5 multiply_reduce_fusion.4
  72.6 0.6 multiply_reduce_fusion.5
  73.4 0.7 constant_dynamic-update-slice_fusion.2
  74.1 1.1 %dynamic-slice_bitcast_fusion.1 = (bf16[3,96,128]{2,1,0:T(8,128)(2,1)S(1)}, bf16[3,96,128]{2,1,0:T(8,128)(2,1)S(1)}, bf16[3,96,128]{2,1,0:T(8,128)(2,1)S(1)}, bf...) fusion(bf16[3,8,96,128]{3,2,1,0:T(8,128)(2,1)} %bitcast.141, ...), kind=kLoop, calls=%fused_computation.47 | loop fusion | bytes 1032220 | tf_op jit(solution)/shard_map/squeeze | solution.py:106
  75.4 1.8 %collective-permute-start.2 = (bf16[3,96,128]{2,1,0:T(8,128)(2,1)S(1)}, bf16[3,96,128]{2,1,0:T(8,128)(2,1)S(1)}, u32[]{:S(2)}, u32[]{:S(2)}) collective-permute-start(bf16[3,96,128]{2,1,0:T(8,128)(2,1)S(1)} %get-tuple-element.197), channel_id=1, source_target_pairs={{0,3},{1,2},{2,1},{3,0},{4,7},{5,6},{6,5},{7,4},{8,11},{9,10},{10,... | collective-permute-start | bytes 221192 | tf_op jit(solution)/shard_map/ppermute | solution.py:107
  77.3 2.5 %collective-permute-start.4 = (bf16[3,96,128]{2,1,0:T(8,128)(2,1)S(1)}, bf16[3,96,128]{2,1,0:T(8,128)(2,1)S(1)}, u32[]{:S(2)}, u32[]{:S(2)}) collective-permute-start(bf16[3,96,128]{2,1,0:T(8,128)(2,1)S(1)} %get-tuple-element.195), channel_id=1, source_target_pairs={{0,5},{1,4},{2,7},{3,6},{4,1},{5,0},{6,3},{7,2},{8,13},{9,12},{10,... | collective-permute-start | bytes 221192 | tf_op jit(solution)/shard_map/ppermute | solution.py:107
  79.8 0.9 bitcast_dynamic-update-slice_fusion.7
  80.7 1.3 %collective-permute-start.5 = (bf16[3,96,128]{2,1,0:T(8,128)(2,1)S(1)}, bf16[3,96,128]{2,1,0:T(8,128)(2,1)S(1)}, u32[]{:S(2)}, u32[]{:S(2)}) collective-permute-start(bf16[3,96,128]{2,1,0:T(8,128)(2,1)S(1)} %get-tuple-element.194), channel_id=1, source_target_pairs={{0,6},{1,7},{2,4},{3,5},{4,2},{5,3},{6,0},{7,1},{8,14},{9,15},{10,... | collective-permute-start | bytes 221192 | tf_op jit(solution)/shard_map/ppermute | solution.py:107
  82.0 2.4 %collective-permute-start.6 = (bf16[3,96,128]{2,1,0:T(8,128)(2,1)S(1)}, bf16[3,96,128]{2,1,0:T(8,128)(2,1)S(1)}, u32[]{:S(2)}, u32[]{:S(2)}) collective-permute-start(bf16[3,96,128]{2,1,0:T(8,128)(2,1)S(1)} %get-tuple-element.193), channel_id=1, source_target_pairs={{0,7},{1,6},{2,5},{3,4},{4,3},{5,2},{6,1},{7,0},{8,15},{9,14},{10,... | collective-permute-start | bytes 221192 | tf_op jit(solution)/shard_map/ppermute | solution.py:107
  84.5 4.7 %collective-permute-done.3 = bf16[3,96,128]{2,1,0:T(8,128)(2,1)S(1)} collective-permute-done((bf16[3,96,128]{2,1,0:T(8,128)(2,1)S(1)}, bf16[3,96,128]{2,1,0:T(8,128)(2,1)S(1)}, u32[]{:S(2)}, u32[]{:S(2)}) %collective-permute-start.3) | collective-permute-done | bytes 73760 | tf_op jit(solution)/shard_map/ppermute | solution.py:107
  89.2 0.9 collective-permute-done.4
  90.2 0.7 gather_fusion
  90.9 1.0 %copy.38 = bf16[1,24,12,8,128]{4,3,1,2,0:T(8,128)(2,1)} copy(bf16[1,24,12,8,128]{4,3,2,1,0:T(8,128)(2,1)S(1)} %bitcast.132) | data formatting | bytes 1179648 | tf_op jit(solution)/shard_map/reshape | solution.py:112
  (67 shorter events, 5.5 us)
Async XLA Ops:
  0.0 42.1 %copy-start = (f32[24,128]{1,0:T(8,128)S(1)}, f32[24,128]{1,0:T(8,128)}, u32[]{:S(2)}) copy-start(f32[24,128]{1,0:T(8,128)} %param.15) | copy-start | bytes 36868
  0.0 8.6 %copy-start.1 = (bf16[1,96,3072]{2,1,0:T(8,128)(2,1)S(1)}, bf16[1,96,3072]{2,1,0:T(8,128)(2,1)}, u32[]{:S(2)}) copy-start(bf16[1,96,3072]{2,1,0:T(8,128)(2,1)} %param.12) | copy-start | bytes 1769476
  2.1 27.4 %copy-start.4 = (u32[32]{0:T(128)S(1)}, u32[32]{0:T(128)}, u32[]{:S(2)}) copy-start(u32[32]{0:T(128)} %constant.115) | copy-start | bytes 388
  2.1 28.7 %copy-start.3 = (s32[24]{0:T(128)S(1)}, s32[24]{0:T(128)}, u32[]{:S(2)}) copy-start(s32[24]{0:T(128)} %param.14) | copy-start | bytes 292
  2.2 38.9 %copy-start.2 = (bf16[1,96,3072]{2,1,0:T(8,128)(2,1)S(1)}, bf16[1,96,3072]{2,1,0:T(8,128)(2,1)}, u32[]{:S(2)}) copy-start(bf16[1,96,3072]{2,1,0:T(8,128)(2,1)} %param.10) | copy-start | bytes 1769476
  2.2 23.2 %all-to-all-start.1 = ((bf16[24,96,128]{2,1,0:T(8,128)(2,1)}), bf16[24,96,128]{2,1,0:T(8,128)(2,1)S(1)}, u32[]{:S(2)}, u32[]{:S(2)}) async-start(bf16[24,96,128]{2,1,0:T(8,128)(2,1)} %copy.23), calls=%async_computation.1 | async-start | bytes 1179648 | tf_op jit(solution)/shard_map/all_to_all | solution.py:80
  25.4 20.2 %all-to-all-start.2 = ((bf16[24,96,128]{2,1,0:T(8,128)(2,1)}), bf16[24,96,128]{2,1,0:T(8,128)(2,1)S(1)}, u32[]{:S(2)}, u32[]{:S(2)}) async-start(bf16[24,96,128]{2,1,0:T(8,128)(2,1)} %copy.25), calls=%async_computation.2 | async-start | bytes 1179648 | tf_op jit(solution)/shard_map/all_to_all | solution.py:81
  45.6 20.2 %all-to-all-start = ((bf16[24,96,128]{2,1,0:T(8,128)(2,1)}), bf16[24,96,128]{2,1,0:T(8,128)(2,1)S(1)}, u32[]{:S(2)}, u32[]{:S(2)}) async-start(bf16[24,96,128]{2,1,0:T(8,128)(2,1)} %copy.21), calls=%async_computation | async-start | bytes 1179648 | tf_op jit(solution)/shard_map/all_to_all | solution.py:79
  75.3 5.4 %collective-permute-start = (bf16[3,96,128]{2,1,0:T(8,128)(2,1)S(1)}, bf16[3,96,128]{2,1,0:T(8,128)(2,1)S(1)}, u32[]{:S(2)}, u32[]{:S(2)}) collective-permute-start(bf16[3,96,128]{2,1,0:T(8,128)(2,1)S(1)} %get-tuple-element.199), channel_id=1, source_target_pairs={{0,1},{1,0},{2,3},{3,2},{4,5},{5,4},{6,7},{7,6},{8,9},{9,8},{10,11... | collective-permute-start | bytes 221192 | tf_op jit(solution)/shard_map/ppermute | solution.py:107
  75.3 6.7 %collective-permute-start.1 = (bf16[3,96,128]{2,1,0:T(8,128)(2,1)S(1)}, bf16[3,96,128]{2,1,0:T(8,128)(2,1)S(1)}, u32[]{:S(2)}, u32[]{:S(2)}) collective-permute-start(bf16[3,96,128]{2,1,0:T(8,128)(2,1)S(1)} %get-tuple-element.198), channel_id=1, source_target_pairs={{0,2},{1,3},{2,0},{3,1},{4,6},{5,7},{6,4},{7,5},{8,10},{9,11},{10,... | collective-permute-start | bytes 221192 | tf_op jit(solution)/shard_map/ppermute | solution.py:107
  75.4 9.0 %collective-permute-start.2 = (bf16[3,96,128]{2,1,0:T(8,128)(2,1)S(1)}, bf16[3,96,128]{2,1,0:T(8,128)(2,1)S(1)}, u32[]{:S(2)}, u32[]{:S(2)}) collective-permute-start(bf16[3,96,128]{2,1,0:T(8,128)(2,1)S(1)} %get-tuple-element.197), channel_id=1, source_target_pairs={{0,3},{1,2},{2,1},{3,0},{4,7},{5,6},{6,5},{7,4},{8,11},{9,10},{10,... | collective-permute-start | bytes 221192 | tf_op jit(solution)/shard_map/ppermute | solution.py:107
  77.2 12.0 %collective-permute-start.3 = (bf16[3,96,128]{2,1,0:T(8,128)(2,1)S(1)}, bf16[3,96,128]{2,1,0:T(8,128)(2,1)S(1)}, u32[]{:S(2)}, u32[]{:S(2)}) collective-permute-start(bf16[3,96,128]{2,1,0:T(8,128)(2,1)S(1)} %get-tuple-element.196), channel_id=1, source_target_pairs={{0,4},{1,5},{2,6},{3,7},{4,0},{5,1},{6,2},{7,3},{8,12},{9,13},{10,... | collective-permute-start | bytes 221192 | tf_op jit(solution)/shard_map/ppermute | solution.py:107
  77.3 12.8 %collective-permute-start.4 = (bf16[3,96,128]{2,1,0:T(8,128)(2,1)S(1)}, bf16[3,96,128]{2,1,0:T(8,128)(2,1)S(1)}, u32[]{:S(2)}, u32[]{:S(2)}) collective-permute-start(bf16[3,96,128]{2,1,0:T(8,128)(2,1)S(1)} %get-tuple-element.195), channel_id=1, source_target_pairs={{0,5},{1,4},{2,7},{3,6},{4,1},{5,0},{6,3},{7,2},{8,13},{9,12},{10,... | collective-permute-start | bytes 221192 | tf_op jit(solution)/shard_map/ppermute | solution.py:107
  80.7 9.4 %collective-permute-start.5 = (bf16[3,96,128]{2,1,0:T(8,128)(2,1)S(1)}, bf16[3,96,128]{2,1,0:T(8,128)(2,1)S(1)}, u32[]{:S(2)}, u32[]{:S(2)}) collective-permute-start(bf16[3,96,128]{2,1,0:T(8,128)(2,1)S(1)} %get-tuple-element.194), channel_id=1, source_target_pairs={{0,6},{1,7},{2,4},{3,5},{4,2},{5,3},{6,0},{7,1},{8,14},{9,15},{10,... | collective-permute-start | bytes 221192 | tf_op jit(solution)/shard_map/ppermute | solution.py:107
  82.0 8.1 %collective-permute-start.6 = (bf16[3,96,128]{2,1,0:T(8,128)(2,1)S(1)}, bf16[3,96,128]{2,1,0:T(8,128)(2,1)S(1)}, u32[]{:S(2)}, u32[]{:S(2)}) collective-permute-start(bf16[3,96,128]{2,1,0:T(8,128)(2,1)S(1)} %get-tuple-element.193), channel_id=1, source_target_pairs={{0,7},{1,6},{2,5},{3,4},{4,3},{5,2},{6,1},{7,0},{8,15},{9,14},{10,... | collective-permute-start | bytes 221192 | tf_op jit(solution)/shard_map/ppermute | solution.py:107
